TPU v7x, 512 devices: a whole 4x8x8 slice. The times are simulated.
512 devices in a mesh: rep: 16 (over y, core), tp: 32 (over z, x).
Axes of the slice: x: 4, y: 8, z: 8, core: 2. Of those that a mesh axis runs over, the one named last changes fastest.
Arguments:
- tokens: bfloat16 [8192, 8192], P('rep', 'tp'), may hold values from -6 to 6
- base_weight: bfloat16 [8192, 8192], P(None, 'tp'), may hold values from -0.0625 to 0.0625
- delta: bfloat16 [48, 64, 2, 128, 128], P('rep', 'tp'), may hold values from -0.375 to 0.375
- live_blocks: int32 [48, 64, 2], P(None, 'tp'), may hold values from 0 to 63, as said below
- row_variant: int32 [8192, 1], P('rep'), may hold values from 0 to 47; in each aligned block of 512 rows (0 to 511, 512 to 1023, ...) at most 21 rows name the same one
Outputs:
- projected: bfloat16 [8192, 8192], P('rep', 'tp')
Inputs may be any that keep to these rules, and one draw needn't show every extreme that they name: `live_blocks`: the 2 block rows listed for one variant and column block are distinct. `row_variant`: among the rows of one index of rep no variant appears more than 21 times, and some variant appears exactly 21 times.
All inputs are finite; a program needn't handle non-finite values.
Results may differ from a plain program's by a relative error of at most 0.0039.
Values may be sent and summed in bfloat16 or wider, within the bound.
A program may use at most 128 MiB of HBM per device.

v0:
```python
import jax
import jax.numpy as jnp
from jax import lax
from jax.sharding import PartitionSpec as P


def multiply(received, weight_tables):
    sources, local_variants, slot_count, feat_width = received.shape
    col_blocks = weight_tables.shape[1]
    block_size = weight_tables.shape[3]
    shaped = received.reshape(
        sources, local_variants, slot_count, col_blocks, feat_width // col_blocks
    )
    flat_weights = weight_tables.reshape(
        local_variants, col_blocks, feat_width // col_blocks, block_size
    )
    result = jnp.einsum(
        "auncf,ucfb->auncb", shaped, flat_weights, preferred_element_type=jnp.float32
    )
    return result.astype(jnp.bfloat16).reshape(
        sources, local_variants, slot_count, col_blocks * block_size
    )


def local(tokens, base_weight, delta, live_blocks, row_variant):
    rep_count = lax.axis_size("rep")
    local_variants = delta.shape[0]
    col_blocks = delta.shape[1]
    live_count = delta.shape[2]
    block_size = delta.shape[3]
    variants = local_variants * rep_count
    row_count = tokens.shape[0]
    capacity = max(2, 2 * row_count // variants)
    feat_width = col_blocks * live_count * block_size
    features_all = lax.all_gather(tokens, "tp", axis=1, tiled=True)
    base_part = jnp.dot(features_all, base_weight, preferred_element_type=jnp.float32)
    variant = row_variant[:, 0]
    onehot = (variant[:, None] == jnp.arange(variants, dtype=jnp.int32)[None, :]).astype(jnp.int32)
    row_rank = jnp.sum((jnp.cumsum(onehot, axis=0) - 1) * onehot, axis=1)
    slot_index = variant * capacity + row_rank
    tile_indices = jnp.take(live_blocks, variant, axis=0).reshape(
        row_count, col_blocks * live_count
    )
    blocks_view = features_all.reshape(row_count, features_all.shape[1] // block_size, block_size)
    picked = jnp.take_along_axis(blocks_view, tile_indices[:, :, None], axis=1).reshape(
        row_count, feat_width
    )
    outgoing = jnp.zeros((variants * capacity, feat_width), jnp.bfloat16).at[slot_index].set(picked)
    all_deltas = lax.all_gather(delta, "rep", axis=0, tiled=True)
    returned = multiply(outgoing.reshape(1, variants, capacity, feat_width), all_deltas)
    returned_flat = returned.reshape(variants * capacity, col_blocks * block_size)
    correction_summand = jnp.take(returned_flat, slot_index, axis=0)
    return (base_part + correction_summand.astype(jnp.float32)).astype(jnp.bfloat16)


def solution(mesh):
    placed = (
        P("rep", "tp"),
        P(None, "tp"),
        P("rep", "tp", None, None, None),
        P(None, "tp", None),
        P("rep", None),
    )
    return jax.shard_map(
        local, mesh=mesh, in_specs=placed, out_specs=P("rep", "tp"), check_vma=False
    )
```

profile of v0, /device:TPU:1, one launch (start us, length us, event | category | flops | bytes accessed | tf_op | source)
XLA Modules:
  0.0 194.5 jit_solution(5336732794186079991)
XLA Ops:
  6.5 0.7 all-gather.3.cloned.1.call-update
  7.3 0.7 all-gather.5.cloned.1.call-update
  8.0 0.7 fusion.9
  8.7 1.2 reduce-window.6
  9.9 0.2 slice_reduce_fusion
  10.2 0.8 copy.20
  11.0 0.8 fusion.8
  11.7 0.7 and_reduce_fusion
  12.5 2.1 %gather_fusion = s32[512,2,2]{2,1,0:T(2,128)S(1)} fusion(s32[48,2,2]{2,1,0:T(2,128)S(1)} %copy.20, s32[1024]{0:T(1024)S(1)} %pad_clamp_fusion.1), kind=kCustom, calls=%fused_computation | custom fusion | bytes 18432 | tf_op jit(solution)/shard_map/jit(_take)/gather | solution.py:41
  14.6 0.2 copy.21
  14.8 0.1 copy.24
  15.0 0.2 reshape.171
  15.2 0.2 copy.22
  15.4 105.8 %all-gather.3.cloned.1.call-done = bf16[512,8192]{1,0:T(8,128)(2,1)} async-done(((bf16[512,256]{1,0:T(8,128)(2,1)}), bf16[512,8192]{1,0:T(8,128)(2,1)}) %all-gather.3.cloned.1.call-update) | async-done | bytes 8388624 | tf_op jit(solution)/shard_map/all_gather | solution.py:35
  121.1 9.3 %copy.28 = bf16[64,8,64,128]{3,2,1,0:T(8,128)(2,1)} copy(bf16[64,8,64,128]{3,1,2,0:T(8,128)(2,1)} %bitcast.50) | data formatting | bytes 16777216
  130.4 24.3 %gather_fusion.2 = bf16[2048,128]{1,0:T(8,128)(2,1)S(1)} fusion(bf16[512,64,128]{2,1,0:T(8,128)(2,1)} %bitcast.48, s32[2048]{0:T(1024)S(1)} %reshape.171), kind=kCustom, calls=%fused_computation.2 | custom fusion | bytes 1064960 | tf_op jit(solution)/shard_map/jit(take_along_axis)/gather | solution.py:45
  154.8 1.6 broadcast_select_fusion
  156.4 2.7 %scatter_custom_fusion = bf16[1008,512]{1,0:T(8,128)(2,1)S(1)} fusion(s32[512]{0:T(512)S(1)} %bitcast.58, bf16[64,8,4,128]{3,2,1,0:T(4,128)(2,1)S(1)} %bitcast.52, bf16[]{:T(256)} %constant.50.clone.1), kind=kCustom, calls=%fused_computation.9 | custom fusion | bytes 1556482 | tf_op jit(solution)/shard_map/scatter | solution.py:48
  159.1 0.2 reshape.153
  159.4 14.4 %all-gather.5.cloned.1.call-done = bf16[48,2,2,128,128]{4,3,2,1,0:T(8,128)(2,1)} async-done(((bf16[3,2,2,128,128]{4,3,2,1,0:T(8,128)(2,1)}), bf16[48,2,2,128,128]{4,3,2,1,0:T(8,128)(2,1)}) %all-gather.5.cloned.1.call-update) | async-done | bytes 6291472 | tf_op jit(solution)/shard_map/all_gather | solution.py:49
  173.8 3.8 %fusion = bf16[1,48,21,2,128]{4,2,3,1,0:T(8,128)(2,1)S(1)} fusion(bf16[48,2,256,128]{3,2,1,0:T(8,128)(2,1)} %bitcast.51, bf16[48,21,2,256]{3,2,1,0:T(2,128)(2,1)S(1)} %reshape.153), kind=kOutput, calls=%fused_computation.5 | convolution fusion | flops 132378624 | bytes 7839744 | tf_op jit(solution)/shard_map/auncf,ucfb->auncb/dot_general | solution.py:17
  177.6 0.4 copy.26
  178.1 2.0 %gather_fusion.1 = bf16[512,256]{1,0:T(8,128)(2,1)S(1)} fusion(bf16[1008,256]{1,0:T(8,128)(2,1)S(1)} %bitcast.49, s32[1024]{0:T(1024)S(1)} %pad_clamp_fusion), kind=kCustom, calls=%fused_computation.1 | custom fusion | bytes 526336 | tf_op jit(solution)/shard_map/jit(_take)/gather | solution.py:52
  180.1 7.6 %fusion.1 = bf16[512,256]{1,0:T(8,128)(2,1)} fusion(bf16[512,8192]{1,0:T(8,128)(2,1)} %all-gather.3.cloned.1.call-done, bf16[8192,256]{1,0:T(8,128)(2,1)} %param.6, bf16[512,256]{1,0:T(8,128)(2,1)S(1)} %gather_fusion.1, pred[512]{0:T(512)(128)(4,1)S(1)} %get-tuple-element.9), kind=kOutput, calls=%fused_computation.7 | convolution fusion | flops 2148007936 | bytes 13107712 | tf_op jit(solution)/shard_map/dot_general | solution.py:36
  (11 shorter events, 0.2 us)
Async XLA Ops:
  6.5 114.6 %all-gather.3.cloned.1.call-start = ((), (), s32[]{:S(2)}) async-start(), calls=%async_computation | async-start | bytes 8650752 | tf_op jit(solution)/shard_map/all_gather | solution.py:35
  7.3 166.5 %all-gather.5.cloned.1.call-start = ((), (), s32[]{:S(2)}) async-start(), calls=%async_computation.1 | async-start | bytes 6684672 | tf_op jit(solution)/shard_map/all_gather | solution.py:49
Sparse Core Ops, SparseCore 0:
  10.4 110.7 all-gather.2
  123.3 50.4 all-gather.4
where the time goes:
time: 195 us
  waiting for transfers between devices  122 us (63%)
  local copies, waits for them, and re-layouts  42.9 us (22%)
  between operations  13.5 us (7%)
  matrix products  11.4 us (6%)
  other arithmetic  5.09 us (3%)
    all_gather x1, waiting for transfers between devices, local(): features_all = lax.all_gather(tokens, 'tp', axis=1, tiled=True)  106 us
    gather x3, local copies, waits for them, and re-layouts, local(): jnp.take_along_axis(blocks_view, tile_indices[:, :, None], axis=1)  24.6 us
    all_gather x1, waiting for transfers between devices, local(): all_deltas = lax.all_gather(delta, 'rep', axis=0, tiled=True)  14.4 us
    unnamed x3, local copies, waits for them, and re-layouts  10.2 us
    dot_general x1, matrix products, local(): jnp.dot(features_all, base_weight, preferred_element_type=jnp.float32)  7.61 us
  transfers between devices with their start and end apart: 2, of which 2 were waited for; matrix products, arithmetic and copies ran while one was open for 23% of the time, Pallas kernels for 0%

commit v1 on v0

--- a/solution.py
+++ b/solution.py
@@ -46,7 +46,25 @@
         row_count, feat_width
     )
     outgoing = jnp.zeros((variants * capacity, feat_width), jnp.bfloat16).at[slot_index].set(picked)
-    all_deltas = lax.all_gather(delta, "rep", axis=0, tiled=True)
+
+    def manage_pieces_all(view):
+        dev_axis = "rep"
+        cores_n = lax.axis_size(dev_axis)
+        tray = [(b, (b + 1) % cores_n) for b in range(cores_n)]
+        cards = [(b, (b - 1) % cores_n) for b in range(cores_n)]
+        clean, big = ([view], [view])
+        for _ in range(cores_n // 2):
+            clean.append(lax.ppermute(clean[-1], dev_axis, tray))
+        for _ in range((cores_n - 1) // 2):
+            big.append(lax.ppermute(big[-1], dev_axis, cards))
+        part_now = jnp.roll(
+            jnp.concatenate([*clean[::-1], *big[1:]], axis=0),
+            (lax.axis_index(dev_axis) - cores_n // 2) * view.shape[0],
+            axis=0,
+        )
+        return part_now
+
+    all_deltas = manage_pieces_all(delta)
     returned = multiply(outgoing.reshape(1, variants, capacity, feat_width), all_deltas)
     returned_flat = returned.reshape(variants * capacity, col_blocks * block_size)
     correction_summand = jnp.take(returned_flat, slot_index, axis=0)

time: 195 us -> 183 us (0.938); the launches traced: 195 us -> 180 us
  waiting for transfers between devices: 122 us -> 31.1 us
  starting transfers between devices: 0.04 us -> 47.8 us
  local copies, waits for them, and re-layouts: 42.9 us -> 68 us
  other arithmetic: 5.09 us -> 8.26 us
    all_gather x1, waiting for transfers between devices: 106 us -> 20.2 us  [local(): features_all = lax.all_gather(tokens, 'tp', axis=1, tiled=True)]
    ppermute x0 -> x15, starting transfers between devices: none -> 47.8 us  [the longest x7 42.6 us: manage_pieces_all(): big.append(lax.ppermute(big[-1], dev_axis, cards))]
    unnamed x3 -> x48, local copies, waits for them, and re-layouts: 10.2 us -> 27.5 us
    all_gather x1 -> x0, waiting for transfers between devices: 14.4 us -> none  [local(): all_deltas = lax.all_gather(delta, 'rep', axis=0, tiled=True)]
    ppermute x0 -> x15, waiting for transfers between devices: none -> 10.1 us  [the longest x8 9.46 us: manage_pieces_all(): clean.append(lax.ppermute(clean[-1], dev_axis, tray))]
    dynamic_slice x0 -> x1, local copies, waits for them, and re-layouts: none -> 4.02 us  [manage_pieces_all(): jnp.roll(jnp.concatenate([*clean[::-1], *big[1:]], axis=0), (lax.axis_ind...]
  transfers between devices with their start and end apart: 2 -> 16, of which waited for: 2 -> 9; matrix products, arithmetic and copies ran while one was open for 23% -> 19% of each run, Pallas kernels for 0% -> 0%
where the time goes in v1:
time: 183 us; the launch traced here: 180 us
  local copies, waits for them, and re-layouts  68 us (37%)
  starting transfers between devices  47.8 us (26%)
  waiting for transfers between devices  31.1 us (17%)
  between operations  13.8 us (8%)
  matrix products  11.3 us (6%)
  other arithmetic  8.26 us (5%)
    ppermute x7, starting transfers between devices, manage_pieces_all(): big.append(lax.ppermute(big[-1], dev_axis, cards))  42.6 us
    unnamed x48, local copies, waits for them, and re-layouts  27.5 us
    gather x3, local copies, waits for them, and re-layouts, local(): jnp.take_along_axis(blocks_view, tile_indices[:, :, None], axis=1)  26.4 us
    all_gather x1, waiting for transfers between devices, local(): features_all = lax.all_gather(tokens, 'tp', axis=1, tiled=True)  20.2 us
    ppermute x8, waiting for transfers between devices, manage_pieces_all(): clean.append(lax.ppermute(clean[-1], dev_axis, tray))  9.46 us
    dot_general x1, matrix products, local(): jnp.dot(features_all, base_weight, preferred_element_type=jnp.float32)  7.61 us
    ppermute x8, starting transfers between devices, manage_pieces_all(): clean.append(lax.ppermute(clean[-1], dev_axis, tray))  5.13 us
    dynamic_slice x1, local copies, waits for them, and re-layouts, manage_pieces_all(): jnp.roll(jnp.concatenate([*clean[::-1], *big[1:]], axis=0), (lax.axis_ind...  4.02 us
  transfers between devices with their start and end apart: 16, of which 9 were waited for; matrix products, arithmetic and copies ran while one was open for 19% of the time, Pallas kernels for 0%

profile of v1, /device:TPU:1, one launch (start us, length us, event | category | flops | bytes accessed | tf_op | source)
XLA Modules:
  0.0 180.3 jit_solution(5013681493526616915)
XLA Ops:
  7.3 2.7 %collective-permute-start = (bf16[3,2,2,128,128]{4,3,2,1,0:T(8,128)(2,1)}, bf16[3,2,2,128,128]{4,3,2,1,0:T(8,128)(2,1)S(1)}, u32[]{:S(2)}, u32[]{:S(2)}) collective-permute-start(bf16[3,2,2,128,128]{4,3,2,1,0:T(8,128)(2,1)} %param.7), channel_id=1, source_target_pairs={{0,32},{32,64},{64,96},{96,128},{128,160},{160,192},{192,224},{224... | collective-permute-start | bytes 1179656 | tf_op jit(solution)/shard_map/ppermute | solution.py:57
  9.9 5.6 %collective-permute-done = bf16[3,2,2,128,128]{4,3,2,1,0:T(8,128)(2,1)S(1)} collective-permute-done((bf16[3,2,2,128,128]{4,3,2,1,0:T(8,128)(2,1)}, bf16[3,2,2,128,128]{4,3,2,1,0:T(8,128)(2,1)S(1)}, u32[]{:S(2)}, u32[]{:S(2)}) %collective-permute-start) | collective-permute-done | bytes 393248 | tf_op jit(solution)/shard_map/ppermute | solution.py:57
  15.5 1.8 %collective-permute-start.1 = (bf16[3,2,2,128,128]{4,3,2,1,0:T(8,128)(2,1)S(1)}, bf16[3,2,2,128,128]{4,3,2,1,0:T(8,128)(2,1)S(1)}, u32[]{:S(2)}, u32[]{:S(2)}) collective-permute-start(bf16[3,2,2,128,128]{4,3,2,1,0:T(8,128)(2,1)S(1)} %collective-permute-done), channel_id=1, source_target_pairs={{0,32},{32,64},{64,96},{96,128},{128,160},{160,192},{192,224},{224... | collective-permute-start | bytes 1179656 | tf_op jit(solution)/shard_map/ppermute | solution.py:57
  17.4 5.4 %collective-permute-start.8 = (bf16[3,2,2,128,128]{4,3,2,1,0:T(8,128)(2,1)}, bf16[3,2,2,128,128]{4,3,2,1,0:T(8,128)(2,1)S(1)}, u32[]{:S(2)}, u32[]{:S(2)}) collective-permute-start(bf16[3,2,2,128,128]{4,3,2,1,0:T(8,128)(2,1)} %param.7), channel_id=1, source_target_pairs={{0,480},{32,0},{64,32},{96,64},{128,96},{160,128},{192,160},{224,1... | collective-permute-start | bytes 1179656 | tf_op jit(solution)/shard_map/ppermute | solution.py:59
  22.7 1.2 collective-permute-done.1
  24.8 6.5 %collective-permute-start.9 = (bf16[3,2,2,128,128]{4,3,2,1,0:T(8,128)(2,1)S(1)}, bf16[3,2,2,128,128]{4,3,2,1,0:T(8,128)(2,1)S(1)}, u32[]{:S(2)}, u32[]{:S(2)}) collective-permute-start(bf16[3,2,2,128,128]{4,3,2,1,0:T(8,128)(2,1)S(1)} %collective-permute-done.8), channel_id=1, source_target_pairs={{0,480},{32,0},{64,32},{96,64},{128,96},{160,128},{192,160},{224,1... | collective-permute-start | bytes 1179656 | tf_op jit(solution)/shard_map/ppermute | solution.py:59
  32.7 7.0 %collective-permute-start.10 = (bf16[3,2,2,128,128]{4,3,2,1,0:T(8,128)(2,1)S(1)}, bf16[3,2,2,128,128]{4,3,2,1,0:T(8,128)(2,1)S(1)}, u32[]{:S(2)}, u32[]{:S(2)}) collective-permute-start(bf16[3,2,2,128,128]{4,3,2,1,0:T(8,128)(2,1)S(1)} %collective-permute-done.9), channel_id=1, source_target_pairs={{0,480},{32,0},{64,32},{96,64},{128,96},{160,128},{192,160},{224,1... | collective-permute-start | bytes 1179656 | tf_op jit(solution)/shard_map/ppermute | solution.py:59
  39.6 1.2 collective-permute-done.3
  41.6 7.2 %collective-permute-start.11 = (bf16[3,2,2,128,128]{4,3,2,1,0:T(8,128)(2,1)S(1)}, bf16[3,2,2,128,128]{4,3,2,1,0:T(8,128)(2,1)}, u32[]{:S(2)}, u32[]{:S(2)}) collective-permute-start(bf16[3,2,2,128,128]{4,3,2,1,0:T(8,128)(2,1)S(1)} %collective-permute-done.10), channel_id=1, source_target_pairs={{0,480},{32,0},{64,32},{96,64},{128,96},{160,128},{192,160},{224,1... | collective-permute-start | bytes 1179656 | tf_op jit(solution)/shard_map/ppermute | solution.py:59
  49.9 1.2 reduce-window.6
  51.4 7.2 %collective-permute-start.12 = (bf16[3,2,2,128,128]{4,3,2,1,0:T(8,128)(2,1)}, bf16[3,2,2,128,128]{4,3,2,1,0:T(8,128)(2,1)}, u32[]{:S(2)}, u32[]{:S(2)}) collective-permute-start(bf16[3,2,2,128,128]{4,3,2,1,0:T(8,128)(2,1)} %collective-permute-done.11), channel_id=1, source_target_pairs={{0,480},{32,0},{64,32},{96,64},{128,96},{160,128},{192,160},{224,1... | collective-permute-start | bytes 1179656 | tf_op jit(solution)/shard_map/ppermute | solution.py:59
  60.2 1.8 %and_reduce_fusion = (pred[512]{0:T(512)(128)(4,1)}, s32[512,1]{0,1:T(1,128)S(1)}, pred[512]{0:T(512)(128)(4,1)}, s32[512,1]{0,1:T(1,128)}) fusion(s32[512,1]{0,1:T(1,128)} %param.9, s32[512,1]{0,1:T(1,128)S(1)} %bitcast.57), kind=kLoop, calls=%fused_computation.63 | loop fusion | flops 7168 | bytes 9216 | tf_op jit(solution)/shard_map/jit(_take)/and | solution.py:41
  62.0 2.1 %gather_fusion = s32[512,2,2]{2,1,0:T(2,128)S(1)} fusion(s32[48,2,2]{2,1,0:T(2,128)S(1)} %copy.12, s32[1024]{0:T(1024)S(1)} %pad_clamp_fusion.1), kind=kCustom, calls=%fused_computation | custom fusion | bytes 18432 | tf_op jit(solution)/shard_map/jit(_take)/gather | solution.py:41
  64.9 6.3 %collective-permute-start.13 = (bf16[3,2,2,128,128]{4,3,2,1,0:T(8,128)(2,1)}, bf16[3,2,2,128,128]{4,3,2,1,0:T(8,128)(2,1)}, u32[]{:S(2)}, u32[]{:S(2)}) collective-permute-start(bf16[3,2,2,128,128]{4,3,2,1,0:T(8,128)(2,1)} %collective-permute-done.12), channel_id=1, source_target_pairs={{0,480},{32,0},{64,32},{96,64},{128,96},{160,128},{192,160},{224,1... | collective-permute-start | bytes 1179656 | tf_op jit(solution)/shard_map/ppermute | solution.py:59
  76.8 3.0 %collective-permute-start.14 = (bf16[3,2,2,128,128]{4,3,2,1,0:T(8,128)(2,1)}, bf16[3,2,2,128,128]{4,3,2,1,0:T(8,128)(2,1)S(1)}, u32[]{:S(2)}, u32[]{:S(2)}) collective-permute-start(bf16[3,2,2,128,128]{4,3,2,1,0:T(8,128)(2,1)} %collective-permute-done.13), channel_id=1, source_target_pairs={{0,480},{32,0},{64,32},{96,64},{128,96},{160,128},{192,160},{224,1... | collective-permute-start | bytes 1179656 | tf_op jit(solution)/shard_map/ppermute | solution.py:59
  96.7 4.0 %constant_dynamic-slice_fusion = bf16[48,2,2,128,128]{4,3,2,1,0:T(8,128)(2,1)} fusion(bf16[96,2,2,128,128]{4,3,2,1,0:T(8,128)(2,1)S(1)} %constant_dynamic-update-slice_fusion, s32[]{:T(128)S(6)} %select_n.81), kind=kLoop, calls=%fused_computation.67 | loop fusion | bytes 12582916 | tf_op jit(solution)/shard_map/jit(_roll_dynamic)/dynamic_slice | solution.py:60
  100.8 20.2 %all-gather.2.cloned.1.call-done = bf16[512,8192]{1,0:T(8,128)(2,1)} async-done(((bf16[512,256]{1,0:T(8,128)(2,1)}), bf16[512,8192]{1,0:T(8,128)(2,1)}) %all-gather.2.cloned.1.call-update) | async-done | bytes 8388624 | tf_op jit(solution)/shard_map/all_gather | solution.py:35
  121.0 9.3 %copy.20 = bf16[64,8,64,128]{3,2,1,0:T(8,128)(2,1)} copy(bf16[64,8,64,128]{3,1,2,0:T(8,128)(2,1)} %bitcast.49) | data formatting | bytes 16777216
  130.3 24.4 %gather_fusion.2 = bf16[2048,128]{1,0:T(8,128)(2,1)S(1)} fusion(bf16[512,64,128]{2,1,0:T(8,128)(2,1)} %bitcast.47, s32[2048]{0:T(1024)S(1)} %reshape.171), kind=kCustom, calls=%fused_computation.2 | custom fusion | bytes 1064960 | tf_op jit(solution)/shard_map/jit(take_along_axis)/gather | solution.py:45
  154.7 1.6 broadcast_select_fusion
  156.3 3.0 %scatter_custom_fusion = bf16[1008,512]{1,0:T(8,128)(2,1)S(1)} fusion(s32[512]{0:T(512)} %bitcast.56, bf16[64,8,4,128]{3,2,1,0:T(4,128)(2,1)S(1)} %bitcast.50, bf16[]{:T(256)} %constant.79.clone.1), kind=kCustom, calls=%fused_computation.9 | custom fusion | bytes 1556992 | tf_op jit(solution)/shard_map/scatter | solution.py:48
  159.6 3.7 %fusion = bf16[1,48,21,2,128]{4,2,3,1,0:T(8,128)(2,1)S(1)} fusion(bf16[48,2,256,128]{3,2,1,0:T(8,128)(2,1)} %bitcast.46, bf16[48,21,2,256]{3,2,1,0:T(2,128)(2,1)S(1)} %reshape.154), kind=kOutput, calls=%fused_computation.5 | convolution fusion | flops 132378624 | bytes 7839744 | tf_op jit(solution)/shard_map/auncf,ucfb->auncb/dot_general | solution.py:17
  163.8 2.0 %gather_fusion.1 = bf16[512,256]{1,0:T(8,128)(2,1)S(1)} fusion(bf16[1008,256]{1,0:T(8,128)(2,1)S(1)} %bitcast.48, s32[1024]{0:T(1024)S(1)} %pad_clamp_fusion), kind=kCustom, calls=%fused_computation.1 | custom fusion | bytes 526336 | tf_op jit(solution)/shard_map/jit(_take)/gather | solution.py:70
  165.8 7.6 %fusion.1 = bf16[512,256]{1,0:T(8,128)(2,1)} fusion(bf16[512,8192]{1,0:T(8,128)(2,1)} %all-gather.2.cloned.1.call-done, bf16[8192,256]{1,0:T(8,128)(2,1)} %param.6, bf16[512,256]{1,0:T(8,128)(2,1)S(1)} %gather_fusion.1, pred[512]{0:T(512)(128)(4,1)S(1)} %copy-done.6), kind=kOutput, calls=%fused_computation.7 | convolution fusion | flops 2148007936 | bytes 13107712 | tf_op jit(solution)/shard_map/dot_general | solution.py:36
  (85 shorter events, 30.4 us)
Async XLA Ops:
  6.5 86.7 %copy-start = (bf16[3,2,2,128,128]{4,3,2,1,0:T(8,128)(2,1)S(1)}, bf16[3,2,2,128,128]{4,3,2,1,0:T(8,128)(2,1)}, u32[]{:S(2)}) copy-start(bf16[3,2,2,128,128]{4,3,2,1,0:T(8,128)(2,1)} %param.7) | copy-start | bytes 1179652
  6.5 114.4 %all-gather.2.cloned.1.call-start = ((), (), s32[]{:S(2)}) async-start(), calls=%async_computation | async-start | bytes 8650752 | tf_op jit(solution)/shard_map/all_gather | solution.py:35
  7.3 8.3 %collective-permute-start = (bf16[3,2,2,128,128]{4,3,2,1,0:T(8,128)(2,1)}, bf16[3,2,2,128,128]{4,3,2,1,0:T(8,128)(2,1)S(1)}, u32[]{:S(2)}, u32[]{:S(2)}) collective-permute-start(bf16[3,2,2,128,128]{4,3,2,1,0:T(8,128)(2,1)} %param.7), channel_id=1, source_target_pairs={{0,32},{32,64},{64,96},{96,128},{128,160},{160,192},{192,224},{224... | collective-permute-start | bytes 1179656 | tf_op jit(solution)/shard_map/ppermute | solution.py:57
  15.5 8.4 %collective-permute-start.1 = (bf16[3,2,2,128,128]{4,3,2,1,0:T(8,128)(2,1)S(1)}, bf16[3,2,2,128,128]{4,3,2,1,0:T(8,128)(2,1)S(1)}, u32[]{:S(2)}, u32[]{:S(2)}) collective-permute-start(bf16[3,2,2,128,128]{4,3,2,1,0:T(8,128)(2,1)S(1)} %collective-permute-done), channel_id=1, source_target_pairs={{0,32},{32,64},{64,96},{96,128},{128,160},{160,192},{192,224},{224... | collective-permute-start | bytes 1179656 | tf_op jit(solution)/shard_map/ppermute | solution.py:57
  17.4 7.4 %collective-permute-start.8 = (bf16[3,2,2,128,128]{4,3,2,1,0:T(8,128)(2,1)}, bf16[3,2,2,128,128]{4,3,2,1,0:T(8,128)(2,1)S(1)}, u32[]{:S(2)}, u32[]{:S(2)}) collective-permute-start(bf16[3,2,2,128,128]{4,3,2,1,0:T(8,128)(2,1)} %param.7), channel_id=1, source_target_pairs={{0,480},{32,0},{64,32},{96,64},{128,96},{160,128},{192,160},{224,1... | collective-permute-start | bytes 1179656 | tf_op jit(solution)/shard_map/ppermute | solution.py:59
  23.9 8.4 %collective-permute-start.2 = (bf16[3,2,2,128,128]{4,3,2,1,0:T(8,128)(2,1)S(1)}, bf16[3,2,2,128,128]{4,3,2,1,0:T(8,128)(2,1)S(1)}, u32[]{:S(2)}, u32[]{:S(2)}) collective-permute-start(bf16[3,2,2,128,128]{4,3,2,1,0:T(8,128)(2,1)S(1)} %collective-permute-done.1), channel_id=1, source_target_pairs={{0,32},{32,64},{64,96},{96,128},{128,160},{160,192},{192,224},{224... | collective-permute-start | bytes 1179656 | tf_op jit(solution)/shard_map/ppermute | solution.py:57
  24.8 7.9 %collective-permute-start.9 = (bf16[3,2,2,128,128]{4,3,2,1,0:T(8,128)(2,1)S(1)}, bf16[3,2,2,128,128]{4,3,2,1,0:T(8,128)(2,1)S(1)}, u32[]{:S(2)}, u32[]{:S(2)}) collective-permute-start(bf16[3,2,2,128,128]{4,3,2,1,0:T(8,128)(2,1)S(1)} %collective-permute-done.8), channel_id=1, source_target_pairs={{0,480},{32,0},{64,32},{96,64},{128,96},{160,128},{192,160},{224,1... | collective-permute-start | bytes 1179656 | tf_op jit(solution)/shard_map/ppermute | solution.py:59
  32.4 8.4 %collective-permute-start.3 = (bf16[3,2,2,128,128]{4,3,2,1,0:T(8,128)(2,1)S(1)}, bf16[3,2,2,128,128]{4,3,2,1,0:T(8,128)(2,1)S(1)}, u32[]{:S(2)}, u32[]{:S(2)}) collective-permute-start(bf16[3,2,2,128,128]{4,3,2,1,0:T(8,128)(2,1)S(1)} %collective-permute-done.2), channel_id=1, source_target_pairs={{0,32},{32,64},{64,96},{96,128},{128,160},{160,192},{192,224},{224... | collective-permute-start | bytes 1179656 | tf_op jit(solution)/shard_map/ppermute | solution.py:57
  32.7 8.3 %collective-permute-start.10 = (bf16[3,2,2,128,128]{4,3,2,1,0:T(8,128)(2,1)S(1)}, bf16[3,2,2,128,128]{4,3,2,1,0:T(8,128)(2,1)S(1)}, u32[]{:S(2)}, u32[]{:S(2)}) collective-permute-start(bf16[3,2,2,128,128]{4,3,2,1,0:T(8,128)(2,1)S(1)} %collective-permute-done.9), channel_id=1, source_target_pairs={{0,480},{32,0},{64,32},{96,64},{128,96},{160,128},{192,160},{224,1... | collective-permute-start | bytes 1179656 | tf_op jit(solution)/shard_map/ppermute | solution.py:59
  40.8 0.8 copy-start.1
  40.8 8.4 %collective-permute-start.4 = (bf16[3,2,2,128,128]{4,3,2,1,0:T(8,128)(2,1)S(1)}, bf16[3,2,2,128,128]{4,3,2,1,0:T(8,128)(2,1)S(1)}, u32[]{:S(2)}, u32[]{:S(2)}) collective-permute-start(bf16[3,2,2,128,128]{4,3,2,1,0:T(8,128)(2,1)S(1)} %collective-permute-done.3), channel_id=1, source_target_pairs={{0,32},{32,64},{64,96},{96,128},{128,160},{160,192},{192,224},{224... | collective-permute-start | bytes 1179656 | tf_op jit(solution)/shard_map/ppermute | solution.py:57
  41.6 9.8 %collective-permute-start.11 = (bf16[3,2,2,128,128]{4,3,2,1,0:T(8,128)(2,1)S(1)}, bf16[3,2,2,128,128]{4,3,2,1,0:T(8,128)(2,1)}, u32[]{:S(2)}, u32[]{:S(2)}) collective-permute-start(bf16[3,2,2,128,128]{4,3,2,1,0:T(8,128)(2,1)S(1)} %collective-permute-done.10), channel_id=1, source_target_pairs={{0,480},{32,0},{64,32},{96,64},{128,96},{160,128},{192,160},{224,1... | collective-permute-start | bytes 1179656 | tf_op jit(solution)/shard_map/ppermute | solution.py:59
  49.2 9.4 %copy-start.3 = (bf16[3,2,2,128,128]{4,3,2,1,0:T(8,128)(2,1)}, bf16[3,2,2,128,128]{4,3,2,1,0:T(8,128)(2,1)S(1)}, u32[]{:S(2)}) copy-start(bf16[3,2,2,128,128]{4,3,2,1,0:T(8,128)(2,1)S(1)} %collective-permute-done.4) | copy-start | bytes 1179652
  49.2 9.4 %collective-permute-start.5 = (bf16[3,2,2,128,128]{4,3,2,1,0:T(8,128)(2,1)S(1)}, bf16[3,2,2,128,128]{4,3,2,1,0:T(8,128)(2,1)}, u32[]{:S(2)}, u32[]{:S(2)}) collective-permute-start(bf16[3,2,2,128,128]{4,3,2,1,0:T(8,128)(2,1)S(1)} %collective-permute-done.4), channel_id=1, source_target_pairs={{0,32},{32,64},{64,96},{96,128},{128,160},{160,192},{192,224},{224... | collective-permute-start | bytes 1179656 | tf_op jit(solution)/shard_map/ppermute | solution.py:57
  51.4 13.6 %collective-permute-start.12 = (bf16[3,2,2,128,128]{4,3,2,1,0:T(8,128)(2,1)}, bf16[3,2,2,128,128]{4,3,2,1,0:T(8,128)(2,1)}, u32[]{:S(2)}, u32[]{:S(2)}) collective-permute-start(bf16[3,2,2,128,128]{4,3,2,1,0:T(8,128)(2,1)} %collective-permute-done.11), channel_id=1, source_target_pairs={{0,480},{32,0},{64,32},{96,64},{128,96},{160,128},{192,160},{224,1... | collective-permute-start | bytes 1179656 | tf_op jit(solution)/shard_map/ppermute | solution.py:59
  58.6 12.6 %collective-permute-start.6 = (bf16[3,2,2,128,128]{4,3,2,1,0:T(8,128)(2,1)}, bf16[3,2,2,128,128]{4,3,2,1,0:T(8,128)(2,1)}, u32[]{:S(2)}, u32[]{:S(2)}) collective-permute-start(bf16[3,2,2,128,128]{4,3,2,1,0:T(8,128)(2,1)} %collective-permute-done.5), channel_id=1, source_target_pairs={{0,32},{32,64},{64,96},{96,128},{128,160},{160,192},{192,224},{224... | collective-permute-start | bytes 1179656 | tf_op jit(solution)/shard_map/ppermute | solution.py:57
  64.3 28.6 %copy-start.4 = (bf16[3,2,2,128,128]{4,3,2,1,0:T(8,128)(2,1)S(1)}, bf16[3,2,2,128,128]{4,3,2,1,0:T(8,128)(2,1)}, u32[]{:S(2)}) copy-start(bf16[3,2,2,128,128]{4,3,2,1,0:T(8,128)(2,1)} %copy-done.3) | copy-start | bytes 1179652
  64.3 28.7 %copy-start.2 = (bf16[3,2,2,128,128]{4,3,2,1,0:T(8,128)(2,1)S(1)}, bf16[3,2,2,128,128]{4,3,2,1,0:T(8,128)(2,1)}, u32[]{:S(2)}) copy-start(bf16[3,2,2,128,128]{4,3,2,1,0:T(8,128)(2,1)} %copy-done.1) | copy-start | bytes 1179652
  64.9 11.8 %collective-permute-start.13 = (bf16[3,2,2,128,128]{4,3,2,1,0:T(8,128)(2,1)}, bf16[3,2,2,128,128]{4,3,2,1,0:T(8,128)(2,1)}, u32[]{:S(2)}, u32[]{:S(2)}) collective-permute-start(bf16[3,2,2,128,128]{4,3,2,1,0:T(8,128)(2,1)} %collective-permute-done.12), channel_id=1, source_target_pairs={{0,480},{32,0},{64,32},{96,64},{128,96},{160,128},{192,160},{224,1... | collective-permute-start | bytes 1179656 | tf_op jit(solution)/shard_map/ppermute | solution.py:59
  71.2 8.6 %collective-permute-start.7 = (bf16[3,2,2,128,128]{4,3,2,1,0:T(8,128)(2,1)}, bf16[3,2,2,128,128]{4,3,2,1,0:T(8,128)(2,1)}, u32[]{:S(2)}, u32[]{:S(2)}) collective-permute-start(bf16[3,2,2,128,128]{4,3,2,1,0:T(8,128)(2,1)} %collective-permute-done.6), channel_id=1, source_target_pairs={{0,32},{32,64},{64,96},{96,128},{128,160},{160,192},{192,224},{224... | collective-permute-start | bytes 1179656 | tf_op jit(solution)/shard_map/ppermute | solution.py:57
  76.8 12.9 %collective-permute-start.14 = (bf16[3,2,2,128,128]{4,3,2,1,0:T(8,128)(2,1)}, bf16[3,2,2,128,128]{4,3,2,1,0:T(8,128)(2,1)S(1)}, u32[]{:S(2)}, u32[]{:S(2)}) collective-permute-start(bf16[3,2,2,128,128]{4,3,2,1,0:T(8,128)(2,1)} %collective-permute-done.13), channel_id=1, source_target_pairs={{0,480},{32,0},{64,32},{96,64},{128,96},{160,128},{192,160},{224,1... | collective-permute-start | bytes 1179656 | tf_op jit(solution)/shard_map/ppermute | solution.py:59
  100.8 53.9 %copy-start.5 = (pred[512,4]{1,0:T(8,128)(4,1)S(1)}, pred[512,4]{1,0:T(8,128)(4,1)}, u32[]{:S(2)}) copy-start(pred[512,4]{1,0:T(8,128)(4,1)} %copy.14) | copy-start | bytes 6148
  130.3 35.5 %copy-start.6 = (pred[512]{0:T(512)(128)(4,1)S(1)}, pred[512]{0:T(512)(128)(4,1)}, u32[]{:S(2)}) copy-start(pred[512]{0:T(512)(128)(4,1)} %get-tuple-element.9) | copy-start | bytes 1540
Sparse Core Ops, SparseCore 0:
  10.4 110.5 all-gather.1
